TPU v7x, 32 devices: a whole 2x2x4 slice. The times are simulated.
32 devices in a mesh: dp: 8 (over z, y), tensor: 4 (over x, core).
Axes of the slice: x: 2, y: 2, z: 4, core: 2. Of those that a mesh axis runs over, the one named last changes fastest.
Arguments:
- tokens: bfloat16 [16384, 768], P(('dp', 'tensor')), may hold values from -6 to 6
- cotangent: bfloat16 [16384, 768], P(('dp', 'tensor')), may hold values from -6 to 6
- segment_ids: int32 [8, 2048], P('dp'), may hold values from 0 to 7, never falling along the last dimension, each value on 1 to 512 neighbouring positions
- ln1_gain: bfloat16 [768], P('dp'), may hold values from 0.5 to 1.5
- ln1_bias: bfloat16 [768], P('dp'), may hold values from -3 to 3
- w_query: bfloat16 [768, 768], P('dp', 'tensor'), may hold values from -0.3125 to 0.3125
- query_bias: bfloat16 [768], P('dp'), may hold values from -3 to 3
- w_key: bfloat16 [768, 768], P('dp', 'tensor'), may hold values from -0.3125 to 0.3125
- w_value: bfloat16 [768, 768], P('dp', 'tensor'), may hold values from -0.21875 to 0.21875
- value_bias: bfloat16 [768], P('dp'), may hold values from -3 to 3
- w_out: bfloat16 [768, 768], P('tensor', 'dp'), may hold values from -0.625 to 0.625
- out_bias: bfloat16 [768], P('dp'), may hold values from -3 to 3
- ln2_gain: bfloat16 [768], P('dp'), may hold values from 0.5 to 1.5
- ln2_bias: bfloat16 [768], P('dp'), may hold values from -3 to 3
- w_in: bfloat16 [768, 3072], P('dp', 'tensor'), may hold values from -0.21875 to 0.21875
- in_bias: bfloat16 [3072], P('dp'), may hold values from -3 to 3
- w_back: bfloat16 [3072, 768], P('tensor', 'dp'), may hold values from -0.15625 to 0.15625
- back_bias: bfloat16 [768], P('dp'), may hold values from -3 to 3
Outputs:
- output: bfloat16 [16384, 768], P(('dp', 'tensor'))
- grad_tokens: float32 [16384, 768], P(('dp', 'tensor'))
- grad_ln1_gain: float32 [768], P('dp')
- grad_ln1_bias: float32 [768], P('dp')
- grad_w_query: float32 [768, 768], P('dp', 'tensor')
- grad_query_bias: float32 [768], P('dp')
- grad_w_key: float32 [768, 768], P('dp', 'tensor')
- grad_w_value: float32 [768, 768], P('dp', 'tensor')
- grad_value_bias: float32 [768], P('dp')
- grad_w_out: float32 [768, 768], P('tensor', 'dp')
- grad_out_bias: float32 [768], P('dp')
- grad_ln2_gain: float32 [768], P('dp')
- grad_ln2_bias: float32 [768], P('dp')
- grad_w_in: float32 [768, 3072], P('dp', 'tensor')
- grad_in_bias: float32 [3072], P('dp')
- grad_w_back: float32 [3072, 768], P('tensor', 'dp')
- grad_back_bias: float32 [768], P('dp')
Inputs may be any that keep to these rules, and one draw needn't show every extreme that they name: `segment_ids`: in each sequence the document numbers never fall; every number 0 to 7 appears, on 1 to 512 consecutive patches, and some document has exactly 512.
All inputs are finite; a program needn't handle non-finite values.
Results may differ from a plain program's by a relative error of at most 0.02.
Values may be sent and summed in bfloat16 or wider, within the bound.
A program may use at most 128 MiB of HBM per device.

v0:
```python
import math
import jax
import jax.numpy as jnp
from jax import lax
from jax.sharding import PartitionSpec as P

HEAD_DIM = 64
EPSILON = 1e-12


def layer_norm(values, gain, shift):
    center = values - jnp.mean(values, axis=-1, keepdims=True)
    spread = jnp.mean(center * center, axis=-1, keepdims=True)
    return center * lax.rsqrt(spread + EPSILON) * gain + shift


def gelu_exact(values):
    return jax.nn.gelu(values, approximate=False)


def contract_rows(left, right):
    return lax.dot_general(
        left, right, (((0,), (0,)), ((), ())), preferred_element_type=jnp.float32
    )


def contract_cols(left, right):
    return lax.dot_general(
        left, right, (((1,), (1,)), ((), ())), preferred_element_type=jnp.float32
    )


def place_slice(length, piece, start):
    return lax.dynamic_update_slice_in_dim(jnp.zeros((length,), jnp.float32), piece, start, 0)


def per_device(
    tokens,
    cotangent,
    segment_ids,
    ln1_gain,
    ln1_bias,
    w_query,
    query_bias,
    w_key,
    w_value,
    value_bias,
    w_out,
    out_bias,
    ln2_gain,
    ln2_bias,
    w_in,
    in_bias,
    w_back,
    back_bias,
):
    f32 = jnp.float32
    bf16 = jnp.bfloat16
    index = lax.axis_index("tensor")
    (
        gain_one,
        shift_one,
        full_query,
        qbias_all,
        full_key,
        full_value,
        vbias_all,
        full_out,
        obias_all,
        gain_two,
        shift_two,
        full_in,
        ibias_all,
        full_back,
        bbias_all,
    ) = (
        lax.all_gather(ln1_gain, "dp", axis=0, tiled=True),
        lax.all_gather(ln1_bias, "dp", axis=0, tiled=True),
        lax.all_gather(w_query, "dp", axis=0, tiled=True),
        lax.all_gather(query_bias, "dp", axis=0, tiled=True),
        lax.all_gather(w_key, "dp", axis=0, tiled=True),
        lax.all_gather(w_value, "dp", axis=0, tiled=True),
        lax.all_gather(value_bias, "dp", axis=0, tiled=True),
        lax.all_gather(w_out, "dp", axis=1, tiled=True),
        lax.all_gather(out_bias, "dp", axis=0, tiled=True),
        lax.all_gather(ln2_gain, "dp", axis=0, tiled=True),
        lax.all_gather(ln2_bias, "dp", axis=0, tiled=True),
        lax.all_gather(w_in, "dp", axis=0, tiled=True),
        lax.all_gather(in_bias, "dp", axis=0, tiled=True),
        lax.all_gather(w_back, "dp", axis=1, tiled=True),
        lax.all_gather(back_bias, "dp", axis=0, tiled=True),
    )
    width = tokens.shape[1]
    head_width = full_query.shape[1]
    hidden_width = full_in.shape[1]
    unit_total = ibias_all.shape[0]
    local_heads = head_width // HEAD_DIM
    scale = HEAD_DIM ** (-0.5)
    gain_one = gain_one.astype(f32)
    shift_one = shift_one.astype(f32)
    gain_two = gain_two.astype(f32)
    shift_two = shift_two.astype(f32)
    query_shift = lax.dynamic_slice_in_dim(qbias_all, index * head_width, head_width).astype(f32)
    value_shift = lax.dynamic_slice_in_dim(vbias_all, index * head_width, head_width).astype(f32)
    unit_shift = lax.dynamic_slice_in_dim(ibias_all, index * hidden_width, hidden_width).astype(f32)
    inputs = tokens.astype(f32)
    act_one = layer_norm(inputs, gain_one, shift_one).astype(bf16)
    group_one = lax.all_gather(act_one, "tensor", axis=0, tiled=True)
    merged = jnp.concatenate([full_query, full_key, full_value], axis=1)
    mixed = jnp.dot(group_one, merged, preferred_element_type=f32)
    group = mixed.shape[0]
    seq_count = segment_ids.shape[0]
    seq_len = segment_ids.shape[1]
    query = (mixed[:, :head_width] + query_shift).astype(bf16).reshape(group, local_heads, HEAD_DIM)
    keys = (
        mixed[:, head_width : 2 * head_width]
        .astype(bf16)
        .reshape(seq_count, seq_len, local_heads, HEAD_DIM)
    )
    values = (
        (mixed[:, 2 * head_width :] + value_shift)
        .astype(bf16)
        .reshape(seq_count, seq_len, local_heads, HEAD_DIM)
    )
    block = math.gcd(512, seq_len)
    per_seq = seq_len // block
    block_count = group // block

    def block_scores(number):
        sequence = number // per_seq
        begin = number * block
        offset = begin - sequence * seq_len
        query_block = lax.dynamic_slice_in_dim(query, begin, block, 0)
        key_seq = lax.dynamic_index_in_dim(keys, sequence, 0, keepdims=False)
        value_seq = lax.dynamic_index_in_dim(values, sequence, 0, keepdims=False)
        doc_all = lax.dynamic_index_in_dim(segment_ids, sequence, 0, keepdims=False)
        doc_rows = lax.dynamic_slice_in_dim(doc_all, offset, block, 0)
        raw = jnp.einsum("qhd,khd->hqk", query_block, key_seq, preferred_element_type=f32)
        same = (doc_rows[:, None] == doc_all[None, :])[None]
        scores = jnp.where(same, raw * scale, -1000000000.0)
        return (scores, query_block, key_seq, value_seq, begin, sequence)

    def forward_block(number):
        scores, query_block, key_seq, value_seq, begin, sequence = block_scores(number)
        top = jnp.max(scores, axis=-1, keepdims=True)
        expo = jnp.exp(scores - top)
        denom = jnp.sum(expo, axis=-1, keepdims=True)
        weights = (expo / denom).astype(bf16)
        result = jnp.einsum("hqk,khd->qhd", weights, value_seq, preferred_element_type=f32)
        return (
            result.reshape(block, head_width).astype(bf16),
            top[..., 0] + jnp.log(denom[..., 0]),
        )

    context_blocks, lse_all = lax.map(forward_block, jnp.arange(block_count))
    context = context_blocks.reshape(group, head_width)
    attn_part = jnp.dot(context, full_out, preferred_element_type=f32).astype(bf16)
    attn_sum = lax.psum_scatter(attn_part, "tensor", scatter_dimension=0, tiled=True).astype(
        jnp.float32
    )
    middle = inputs + attn_sum + obias_all.astype(f32)
    act_two = layer_norm(middle, gain_two, shift_two).astype(bf16)
    group_two = lax.all_gather(act_two, "tensor", axis=0, tiled=True)
    pre = jnp.dot(group_two, full_in, preferred_element_type=f32) + unit_shift
    hidden = gelu_exact(pre).astype(bf16)
    mlp_part = jnp.dot(hidden, full_back, preferred_element_type=f32).astype(bf16)
    mlp_sum = lax.psum_scatter(mlp_part, "tensor", scatter_dimension=0, tiled=True).astype(
        jnp.float32
    )
    result = middle + mlp_sum + bbias_all.astype(f32)
    output = result.astype(bf16)
    back_query, back_key, back_value, back_out, back_in, back_back = (
        lax.all_gather(w_query, "dp", axis=0, tiled=True),
        lax.all_gather(w_key, "dp", axis=0, tiled=True),
        lax.all_gather(w_value, "dp", axis=0, tiled=True),
        lax.all_gather(w_out, "dp", axis=1, tiled=True),
        lax.all_gather(w_in, "dp", axis=0, tiled=True),
        lax.all_gather(w_back, "dp", axis=1, tiled=True),
    )
    merged_back = jnp.concatenate([back_query, back_key, back_value], axis=1)
    upstream = cotangent.astype(f32)
    back_bias_term = jnp.sum(upstream, axis=0)
    cot_rows = lax.all_gather(cotangent, "tensor", axis=0, tiled=True)
    grad_w_back = contract_rows(hidden, cot_rows)
    grad_hidden = contract_cols(cot_rows, back_back)
    gelu_out, gelu_pull = jax.vjp(gelu_exact, pre)
    grad_pre = gelu_pull(grad_hidden)[0]
    unit_term = jnp.sum(grad_pre, axis=0)
    pre_low = grad_pre.astype(bf16)
    grad_w_in = contract_rows(group_two, pre_low)
    grad_norm_two = lax.psum_scatter(
        contract_cols(pre_low, back_in).astype(jnp.bfloat16),
        "tensor",
        scatter_dimension=0,
        tiled=True,
    ).astype(jnp.float32)
    norm_out, norm_pull = jax.vjp(layer_norm, middle, gain_two, shift_two)
    grad_mid_norm, ln2_gain_term, ln2_bias_term = norm_pull(grad_norm_two)
    grad_middle = upstream + grad_mid_norm
    out_bias_term = jnp.sum(grad_middle, axis=0)
    middle_low = grad_middle.astype(bf16)
    middle_rows = lax.all_gather(middle_low, "tensor", axis=0, tiled=True)
    grad_w_out = contract_rows(context, middle_rows)
    grad_context = (
        contract_cols(middle_rows, back_out).astype(bf16).reshape(group, local_heads, HEAD_DIM)
    )

    def backward_block(carry, number):
        keys_acc, values_acc = carry
        scores, query_block, key_seq, value_seq, begin, sequence = block_scores(number)
        lse = lax.dynamic_index_in_dim(lse_all, number, 0, keepdims=False)
        probs = jnp.exp(scores - lse[:, :, None])
        weights = probs.astype(bf16)
        upstream_block = lax.dynamic_slice_in_dim(grad_context, begin, block, 0)
        grad_weights = jnp.einsum(
            "qhd,khd->hqk", upstream_block, value_seq, preferred_element_type=f32
        )
        delta = jnp.sum(grad_weights * probs, axis=-1, keepdims=True)
        grad_raw = (probs * (grad_weights - delta) * scale).astype(bf16)
        query_part = jnp.einsum("hqk,khd->qhd", grad_raw, key_seq, preferred_element_type=f32)
        key_part = jnp.einsum("hqk,qhd->khd", grad_raw, query_block, preferred_element_type=f32)
        value_part = jnp.einsum("hqk,qhd->khd", weights, upstream_block, preferred_element_type=f32)
        keys_acc = lax.dynamic_update_index_in_dim(
            keys_acc,
            lax.dynamic_index_in_dim(keys_acc, sequence, 0, keepdims=False) + key_part,
            sequence,
            0,
        )
        values_acc = lax.dynamic_update_index_in_dim(
            values_acc,
            lax.dynamic_index_in_dim(values_acc, sequence, 0, keepdims=False) + value_part,
            sequence,
            0,
        )
        return ((keys_acc, values_acc), query_part)

    empty = jnp.zeros((seq_count, seq_len, local_heads, HEAD_DIM), f32)
    (grad_keys, grad_values), query_parts = lax.scan(
        backward_block, (empty, empty), jnp.arange(block_count)
    )
    grad_query = query_parts.reshape(group, head_width)
    grad_keys = grad_keys.reshape(group, head_width)
    grad_values = grad_values.reshape(group, head_width)
    query_term = jnp.sum(grad_query, axis=0)
    value_term = jnp.sum(grad_values, axis=0)
    grad_lows = jnp.concatenate([grad_query, grad_keys, grad_values], axis=1).astype(bf16)
    grad_merged = contract_rows(group_one, grad_lows)
    grad_w_query = grad_merged[:, :head_width]
    grad_w_key = grad_merged[:, head_width : 2 * head_width]
    grad_w_value = grad_merged[:, 2 * head_width :]
    grad_norm_one = lax.psum_scatter(
        contract_cols(grad_lows, merged_back).astype(jnp.bfloat16),
        "tensor",
        scatter_dimension=0,
        tiled=True,
    ).astype(jnp.float32)
    first_out, first_pull = jax.vjp(layer_norm, inputs, gain_one, shift_one)
    grad_in_norm, ln1_gain_term, ln1_bias_term = first_pull(grad_norm_one)
    grad_tokens = grad_middle + grad_in_norm
    vectors = (
        lax.psum(ln1_gain_term.astype(jnp.bfloat16), "tensor").astype(jnp.float32),
        lax.psum(ln1_bias_term.astype(jnp.bfloat16), "tensor").astype(jnp.float32),
        lax.psum(
            place_slice(width, query_term, index * head_width).astype(jnp.bfloat16), "tensor"
        ).astype(jnp.float32),
        lax.psum(
            place_slice(width, value_term, index * head_width).astype(jnp.bfloat16), "tensor"
        ).astype(jnp.float32),
        lax.psum(out_bias_term.astype(jnp.bfloat16), "tensor").astype(jnp.float32),
        lax.psum(ln2_gain_term.astype(jnp.bfloat16), "tensor").astype(jnp.float32),
        lax.psum(ln2_bias_term.astype(jnp.bfloat16), "tensor").astype(jnp.float32),
        lax.psum(
            place_slice(unit_total, unit_term, index * hidden_width).astype(jnp.bfloat16), "tensor"
        ).astype(jnp.float32),
        lax.psum(back_bias_term.astype(jnp.bfloat16), "tensor").astype(jnp.float32),
    )
    (
        grad_w_query,
        grad_w_key,
        grad_w_value,
        grad_w_out,
        grad_w_in,
        grad_w_back,
        grad_ln1_gain,
        grad_ln1_bias,
        grad_query_bias,
        grad_value_bias,
        grad_out_bias,
        grad_ln2_gain,
        grad_ln2_bias,
        grad_in_bias,
        grad_back_bias,
    ) = (
        lax.psum_scatter(grad_w_query, "dp", scatter_dimension=0, tiled=True),
        lax.psum_scatter(grad_w_key, "dp", scatter_dimension=0, tiled=True),
        lax.psum_scatter(grad_w_value, "dp", scatter_dimension=0, tiled=True),
        lax.psum_scatter(grad_w_out, "dp", scatter_dimension=1, tiled=True),
        lax.psum_scatter(grad_w_in, "dp", scatter_dimension=0, tiled=True),
        lax.psum_scatter(grad_w_back, "dp", scatter_dimension=1, tiled=True),
        lax.psum_scatter(vectors[0], "dp", scatter_dimension=0, tiled=True),
        lax.psum_scatter(vectors[1], "dp", scatter_dimension=0, tiled=True),
        lax.psum_scatter(vectors[2], "dp", scatter_dimension=0, tiled=True),
        lax.psum_scatter(vectors[3], "dp", scatter_dimension=0, tiled=True),
        lax.psum_scatter(vectors[4], "dp", scatter_dimension=0, tiled=True),
        lax.psum_scatter(vectors[5], "dp", scatter_dimension=0, tiled=True),
        lax.psum_scatter(vectors[6], "dp", scatter_dimension=0, tiled=True),
        lax.psum_scatter(vectors[7], "dp", scatter_dimension=0, tiled=True),
        lax.psum_scatter(vectors[8], "dp", scatter_dimension=0, tiled=True),
    )
    return (
        output,
        grad_tokens,
        grad_ln1_gain,
        grad_ln1_bias,
        grad_w_query,
        grad_query_bias,
        grad_w_key,
        grad_w_value,
        grad_value_bias,
        grad_w_out,
        grad_out_bias,
        grad_ln2_gain,
        grad_ln2_bias,
        grad_w_in,
        grad_in_bias,
        grad_w_back,
        grad_back_bias,
    )


def solution(mesh):
    return jax.shard_map(
        per_device,
        mesh=mesh,
        in_specs=(
            P(("dp", "tensor"), None),
            P(("dp", "tensor"), None),
            P("dp", None),
            P("dp"),
            P("dp"),
            P("dp", "tensor"),
            P("dp"),
            P("dp", "tensor"),
            P("dp", "tensor"),
            P("dp"),
            P("tensor", "dp"),
            P("dp"),
            P("dp"),
            P("dp"),
            P("dp", "tensor"),
            P("dp"),
            P("tensor", "dp"),
            P("dp"),
        ),
        out_specs=(
            P(("dp", "tensor"), None),
            P(("dp", "tensor"), None),
            P("dp"),
            P("dp"),
            P("dp", "tensor"),
            P("dp"),
            P("dp", "tensor"),
            P("dp", "tensor"),
            P("dp"),
            P("tensor", "dp"),
            P("dp"),
            P("dp"),
            P("dp"),
            P("dp", "tensor"),
            P("dp"),
            P("tensor", "dp"),
            P("dp"),
        ),
        check_vma=False,
    )
```

profile of v0, /device:TPU:0, one launch (start us, length us, event | category | flops | bytes accessed | tf_op | source)
XLA Modules:
  0.0 1247.8 jit_solution(12022204815762069830)
XLA Ops:
  19.7 39.5 %all-reduce.18 = (bf16[768]{0:T(1024)(128)(2,1)S(1)}, bf16[768]{0:T(1024)(128)(2,1)S(1)}, bf16[768]{0:T(1024)(128)(2,1)S(1)}, bf16[768]{0:T(1024)(128)(2,1)S(1)}...) all-reduce(bf16[768]{0:T(1024)(128)(2,1)S(1)} %dynamic-update-slice, ...), channel_id=1, replica_groups=mesh['dp'=8,'tensor'=4] {'dp'}, use_global_device_ids=true, to_apply=%add.1 | all-reduce | flops 6144 | bytes 24576
  62.5 31.0 %all_gather.71 = bf16[192,768]{0,1:T(8,128)(2,1)S(1)} all-gather(bf16[192,96]{0,1:T(8,128)(2,1)S(1)} %copy.44), channel_id=1, replica_groups=mesh['dp'=8,'tensor'=4] {'dp'}, dimensions={1}, use_global_device_ids=true | all-gather | bytes 331776 | tf_op jit(solution)/shard_map/all_gather | solution.py:84
  93.5 31.0 %all_gather.66 = bf16[768,192]{1,0:T(8,128)(2,1)S(1)} all-gather(bf16[96,192]{1,0:T(8,128)(2,1)S(1)} %copy-done.36), channel_id=1, replica_groups=mesh['dp'=8,'tensor'=4] {'dp'}, dimensions={0}, use_global_device_ids=true | all-gather | bytes 331776 | tf_op jit(solution)/shard_map/all_gather | solution.py:79
  124.5 31.0 %all_gather.67 = bf16[768,192]{1,0:T(8,128)(2,1)S(1)} all-gather(bf16[96,192]{1,0:T(8,128)(2,1)S(1)} %copy-done.37), channel_id=1, replica_groups=mesh['dp'=8,'tensor'=4] {'dp'}, dimensions={0}, use_global_device_ids=true | all-gather | bytes 331776 | tf_op jit(solution)/shard_map/all_gather | solution.py:81
  155.5 31.1 %all_gather.68 = bf16[768,192]{1,0:T(8,128)(2,1)S(1)} all-gather(bf16[96,192]{1,0:T(8,128)(2,1)S(1)} %copy-done.38), channel_id=1, replica_groups=mesh['dp'=8,'tensor'=4] {'dp'}, dimensions={0}, use_global_device_ids=true | all-gather | bytes 331776 | tf_op jit(solution)/shard_map/all_gather | solution.py:82
  191.6 98.7 %while.30 = (s32[]{:T(128)}, bf16[4,512,192]{1,2,0:T(8,128)(2,1)}, f32[4,3,512]{2,1,0:T(4,128)S(1)}, s32[4]{0:T(128)S(1)}, s32[1,2048]{1,0:T(1,128)S(1)}, /*inde...) while((s32[]{:T(128)}, bf16[4,512,192]{1,2,0:T(8,128)(2,1)}, ...), condition=%wide.region_5.6_spmd, body=%wide.region_2.5_spmd.sunk | while | flops 844200448 | bytes 44372400 | solution.py:155
  202.1 6.8 fusion.178
  208.8 6.7 fusion.179
  226.8 6.8 fusion.178
  233.5 6.7 fusion.179
  251.4 6.8 fusion.178
  258.2 6.7 fusion.179
  276.1 6.8 fusion.178
  282.9 6.7 fusion.179
  296.1 34.7 %reduce-scatter.19.cloned.1.call-done = bf16[512,768]{1,0:T(8,128)(2,1)} async-done(((bf16[2048,768]{1,0:T(8,128)(2,1)}), bf16[512,768]{1,0:T(8,128)(2,1)}) %reduce-scatter.19.cloned.1.call-update) | async-done | bytes 786448 | tf_op jit(solution)/shard_map/reduce_scatter | solution.py:158
  336.7 26.4 %all-gather = bf16[8,1,384]{2,1,0:T(2,128)(2,1)S(1)} all-gather(bf16[1,1,384]{2,1,0:T(2,128)(2,1)S(1)} %reshape.282), channel_id=1, replica_groups=mesh['dp'=8,'tensor'=4] {'dp'}, dimensions={0}, use_global_device_ids=true | all-gather | bytes 6912 | tf_op jit(solution)/shard_map/all_gather | solution.py:89
  366.1 7.6 fusion.135
  373.6 36.3 %all-gather.14.cloned.1.call-done = bf16[768,768]{0,1:T(8,128)(2,1)} async-done(((bf16[768,96]{0,1:T(8,128)(2,1)}), bf16[768,768]{0,1:T(8,128)(2,1)}) %all-gather.14.cloned.1.call-update) | async-done | bytes 1179664 | tf_op jit(solution)/shard_map/all_gather | solution.py:90
  409.9 28.5 %all-gather.16.cloned.1.call-done = bf16[2048,768]{1,0:T(8,128)(2,1)} async-done(((bf16[512,768]{1,0:T(8,128)(2,1)}), bf16[2048,768]{1,0:T(8,128)(2,1)}) %all-gather.16.cloned.1.call-update) | async-done | bytes 3145744 | tf_op jit(solution)/shard_map/all_gather | solution.py:183
  438.5 20.5 %fusion.128 = (bf16[768]{0:T(1024)(128)(2,1)}, bf16[2048,768]{1,0:T(8,128)(2,1)S(1)}, f32[2048,768]{1,0:T(8,128)}) fusion(f32[2048,768]{1,0:T(8,128)} %fusion.135, f32[768]{0:T(1024)S(1)} %dynamic-slice_convert_fusion, bf16[2048,768]{1,0:T(8,128)(2,1)} %all-gather.16.cloned.1.call-done, bf16[768,768]{0,1:T(8,128)(2,1)} %all-gather.14.cloned.1.call-done), kind=kOutput, calls=%fused_computation.153 | convolution fusion | flops 2532310272 | bytes 20058624 | tf_op jit(solution)/shard_map/dot_general | solution.py:28
  476.8 26.1 %reduce-scatter.23.cloned.1.call-done = bf16[512,768]{1,0:T(8,128)(2,1)} async-done(((bf16[2048,768]{1,0:T(8,128)(2,1)}), bf16[512,768]{1,0:T(8,128)(2,1)}) %reduce-scatter.23.cloned.1.call-update) | async-done | bytes 786448 | tf_op jit(solution)/shard_map/reduce_scatter | solution.py:191
  507.4 35.9 %reduce-scatter.21.cloned.1.call-done = bf16[512,768]{1,0:T(8,128)(2,1)} async-done(((bf16[2048,768]{1,0:T(8,128)(2,1)}), bf16[512,768]{1,0:T(8,128)(2,1)}) %reduce-scatter.21.cloned.1.call-update) | async-done | bytes 786448 | tf_op jit(solution)/shard_map/reduce_scatter | solution.py:167
  549.5 28.4 %all-gather.18.cloned.1.call-done = bf16[2048,768]{1,0:T(8,128)(2,1)} async-done(((bf16[512,768]{1,0:T(8,128)(2,1)}), bf16[2048,768]{1,0:T(8,128)(2,1)}) %all-gather.18.cloned.1.call-update) | async-done | bytes 3145744 | tf_op jit(solution)/shard_map/all_gather | solution.py:202
  588.9 258.0 %while.31 = (s32[]{:T(128)}, f32[1,2048,3,64]{1,3,2,0:T(8,128)}, f32[1,2048,3,64]{1,3,2,0:T(8,128)}, f32[4,512,3,64]{1,3,2,0:T(8,128)}, s32[4]{0:T(128)S(1)}, /*...) while((s32[]{:T(128)}, f32[1,2048,3,64]{1,3,2,0:T(8,128)}, ...), condition=%wide.region_15.16_spmd, body=%wide.region_13.15_spmd.sunk | while | flops 2096897024 | bytes 208079408 | solution.py:238
  596.7 7.2 fusion.193
  604.0 6.3 fusion.190
  610.3 20.9 %fusion.194 = f32[4,512,3,64]{1,3,2,0:T(8,128)} fusion(f32[4,512,3,64]{1,3,2,0:T(8,128)} %get-tuple-element.595, s32[]{:T(128)S(6)} %copy.83, f32[3,512,2048]{2,1,0:T(8,128)} %fusion.190, f32[3,512,2048]{2,1,0:T(8,128)} %copy-done, f32[3,512]{1,0:T(4,128)S(1)} %dynamic-slice_bitcast_fusion.2, pred[512,2048]{1,0:T(8,128)(4,1)S(1)} %broadcast_compare_fusion.5, ...), kind=kOutput, calls=%fused_computation.44.clone.1 | convolution fusion | flops 437259776 | bytes 53624836 | tf_op jit(solution)/shard_map/while/body/eval_jaxpr/hqk,khd->qhd/dot_general | solution.py:220
  631.2 22.6 %fusion.192 = f32[1,2048,3,64]{1,3,2,0:T(8,128)} fusion(f32[3,512,2048]{2,1,0:T(8,128)} %fusion.190, f32[3,512,2048]{2,1,0:T(8,128)} %copy-done, f32[3,512]{1,0:T(4,128)S(1)} %dynamic-slice_bitcast_fusion.2, pred[512,2048]{1,0:T(8,128)(4,1)S(1)} %broadcast_compare_fusion.5, f32[1,2048,3,64]{1,3,2,0:T(8,128)} %get-tuple-element.593, ...), kind=kOutput, calls=%fused_computation.39.clone.1 | convolution fusion | flops 437652992 | bytes 55787524 | tf_op jit(solution)/shard_map/while/body/eval_jaxpr/hqk,qhd->khd/dot_general | solution.py:221
  661.5 7.2 fusion.193
  668.7 6.3 fusion.190
  675.0 20.7 %fusion.194 = f32[4,512,3,64]{1,3,2,0:T(8,128)} fusion(f32[4,512,3,64]{1,3,2,0:T(8,128)} %get-tuple-element.595, s32[]{:T(128)S(6)} %copy.83, f32[3,512,2048]{2,1,0:T(8,128)} %fusion.190, f32[3,512,2048]{2,1,0:T(8,128)} %copy-done, f32[3,512]{1,0:T(4,128)S(1)} %dynamic-slice_bitcast_fusion.2, pred[512,2048]{1,0:T(8,128)(4,1)S(1)} %broadcast_compare_fusion.5, ...), kind=kOutput, calls=%fused_computation.44.clone.1 | convolution fusion | flops 437259776 | bytes 53624836 | tf_op jit(solution)/shard_map/while/body/eval_jaxpr/hqk,khd->qhd/dot_general | solution.py:220
  695.7 22.4 %fusion.192 = f32[1,2048,3,64]{1,3,2,0:T(8,128)} fusion(f32[3,512,2048]{2,1,0:T(8,128)} %fusion.190, f32[3,512,2048]{2,1,0:T(8,128)} %copy-done, f32[3,512]{1,0:T(4,128)S(1)} %dynamic-slice_bitcast_fusion.2, pred[512,2048]{1,0:T(8,128)(4,1)S(1)} %broadcast_compare_fusion.5, f32[1,2048,3,64]{1,3,2,0:T(8,128)} %get-tuple-element.593, ...), kind=kOutput, calls=%fused_computation.39.clone.1 | convolution fusion | flops 437652992 | bytes 55787524 | tf_op jit(solution)/shard_map/while/body/eval_jaxpr/hqk,qhd->khd/dot_general | solution.py:221
  725.8 7.2 fusion.193
  739.2 20.7 %fusion.194 = f32[4,512,3,64]{1,3,2,0:T(8,128)} fusion(f32[4,512,3,64]{1,3,2,0:T(8,128)} %get-tuple-element.595, s32[]{:T(128)S(6)} %copy.83, f32[3,512,2048]{2,1,0:T(8,128)} %fusion.190, f32[3,512,2048]{2,1,0:T(8,128)} %copy-done, f32[3,512]{1,0:T(4,128)S(1)} %dynamic-slice_bitcast_fusion.2, pred[512,2048]{1,0:T(8,128)(4,1)S(1)} %broadcast_compare_fusion.5, ...), kind=kOutput, calls=%fused_computation.44.clone.1 | convolution fusion | flops 437259776 | bytes 53624836 | tf_op jit(solution)/shard_map/while/body/eval_jaxpr/hqk,khd->qhd/dot_general | solution.py:220
  760.0 22.4 %fusion.192 = f32[1,2048,3,64]{1,3,2,0:T(8,128)} fusion(f32[3,512,2048]{2,1,0:T(8,128)} %fusion.190, f32[3,512,2048]{2,1,0:T(8,128)} %copy-done, f32[3,512]{1,0:T(4,128)S(1)} %dynamic-slice_bitcast_fusion.2, pred[512,2048]{1,0:T(8,128)(4,1)S(1)} %broadcast_compare_fusion.5, f32[1,2048,3,64]{1,3,2,0:T(8,128)} %get-tuple-element.593, ...), kind=kOutput, calls=%fused_computation.39.clone.1 | convolution fusion | flops 437652992 | bytes 55787524 | tf_op jit(solution)/shard_map/while/body/eval_jaxpr/hqk,qhd->khd/dot_general | solution.py:221
  790.1 7.2 fusion.193
  797.3 6.3 fusion.190
  803.6 20.8 %fusion.194 = f32[4,512,3,64]{1,3,2,0:T(8,128)} fusion(f32[4,512,3,64]{1,3,2,0:T(8,128)} %get-tuple-element.595, s32[]{:T(128)S(6)} %copy.83, f32[3,512,2048]{2,1,0:T(8,128)} %fusion.190, f32[3,512,2048]{2,1,0:T(8,128)} %copy-done, f32[3,512]{1,0:T(4,128)S(1)} %dynamic-slice_bitcast_fusion.2, pred[512,2048]{1,0:T(8,128)(4,1)S(1)} %broadcast_compare_fusion.5, ...), kind=kOutput, calls=%fused_computation.44.clone.1 | convolution fusion | flops 437259776 | bytes 53624836 | tf_op jit(solution)/shard_map/while/body/eval_jaxpr/hqk,khd->qhd/dot_general | solution.py:220
  824.3 22.4 %fusion.192 = f32[1,2048,3,64]{1,3,2,0:T(8,128)} fusion(f32[3,512,2048]{2,1,0:T(8,128)} %fusion.190, f32[3,512,2048]{2,1,0:T(8,128)} %copy-done, f32[3,512]{1,0:T(4,128)S(1)} %dynamic-slice_bitcast_fusion.2, pred[512,2048]{1,0:T(8,128)(4,1)S(1)} %broadcast_compare_fusion.5, f32[1,2048,3,64]{1,3,2,0:T(8,128)} %get-tuple-element.593, ...), kind=kOutput, calls=%fused_computation.39.clone.1 | convolution fusion | flops 437652992 | bytes 55787524 | tf_op jit(solution)/shard_map/while/body/eval_jaxpr/hqk,qhd->khd/dot_general | solution.py:221
  866.8 7.5 fusion.114
  887.3 9.5 reduce-scatter.25.cloned.1.call-done
  901.8 10.3 all-reduce.19
  912.1 38.8 %all-reduce.17 = (f32[768]{0:T(1024)S(1)}, f32[768]{0:T(1024)S(1)}, f32[768]{0:T(1024)S(1)}, f32[768]{0:T(1024)S(1)}, f32[768]{0:T(1024)S(1)}, /*index=5*/f32[76...) all-reduce(bf16[768]{0:T(1024)(128)(2,1)S(1)} %get-tuple-element.37, ...), channel_id=6, replica_groups=mesh['dp'=8,'tensor'=4] {'dp'}, use_global_device_ids=true, to_apply=%region_21.22.clone | all-reduce | flops 9216 | bytes 55296
  958.0 12.7 %reduce-scatter.29.cloned.1.call-done = f32[768,96]{0,1:T(8,128)} async-done(((f32[768,768]{0,1:T(8,128)}), f32[768,96]{0,1:T(8,128)}) %reduce-scatter.29.cloned.1.call-update) | async-done | bytes 294928 | tf_op jit(solution)/shard_map/reduce_scatter | solution.py:299
  970.7 72.6 %reduce-scatter.27.cloned.1.call-done = f32[96,768]{1,0:T(8,128)} async-done(((f32[768,768]{1,0:T(8,128)}), f32[96,768]{1,0:T(8,128)}) %reduce-scatter.27.cloned.1.call-update) | async-done | bytes 294928 | tf_op jit(solution)/shard_map/reduce_scatter | solution.py:298
  1043.2 65.9 %reduce-scatter.35.cloned.1.call-done = f32[96,192]{1,0:T(8,128)} async-done(((f32[768,192]{1,0:T(8,128)}), f32[96,192]{1,0:T(8,128)}) %reduce-scatter.35.cloned.1.call-update) | async-done | bytes 73744
  1109.2 65.4 %reduce-scatter.33.cloned.1.call-done = f32[96,192]{1,0:T(8,128)} async-done(((f32[768,192]{1,0:T(8,128)}), f32[96,192]{1,0:T(8,128)}) %reduce-scatter.33.cloned.1.call-update) | async-done | bytes 73744
  1174.5 65.9 %reduce-scatter.31.cloned.1.call-done = f32[96,192]{1,0:T(8,128)} async-done(((f32[768,192]{1,0:T(8,128)}), f32[96,192]{1,0:T(8,128)}) %reduce-scatter.31.cloned.1.call-update) | async-done | bytes 73744
  (297 shorter events, 166.8 us)
Async XLA Ops:
  8.0 54.3 %copy-start.39 = (bf16[192,96]{1,0:T(8,128)(2,1)S(1)}, bf16[192,96]{1,0:T(8,128)(2,1)}, u32[]{:S(2)}) copy-start(bf16[192,96]{1,0:T(8,128)(2,1)} %param.32) | copy-start | bytes 110596
  8.0 85.5 %copy-start.36 = (bf16[96,192]{1,0:T(8,128)(2,1)S(1)}, bf16[96,192]{1,0:T(8,128)(2,1)}, u32[]{:S(2)}) copy-start(bf16[96,192]{1,0:T(8,128)(2,1)} %param.27) | copy-start | bytes 110596
  8.0 116.4 %copy-start.37 = (bf16[96,192]{1,0:T(8,128)(2,1)S(1)}, bf16[96,192]{1,0:T(8,128)(2,1)}, u32[]{:S(2)}) copy-start(bf16[96,192]{1,0:T(8,128)(2,1)} %param.29) | copy-start | bytes 110596
  8.1 147.4 %copy-start.38 = (bf16[96,192]{1,0:T(8,128)(2,1)S(1)}, bf16[96,192]{1,0:T(8,128)(2,1)}, u32[]{:S(2)}) copy-start(bf16[96,192]{1,0:T(8,128)(2,1)} %param.30) | copy-start | bytes 110596
  8.1 178.5 %all-gather.8.cloned.1.call-start = ((), (), s32[]{:S(2)}) async-start(), calls=%async_computation.10 | async-start | bytes 3932160 | tf_op jit(solution)/shard_map/all_gather | solution.py:108
  9.4 52.8 %copy-start.34 = (f32[512]{0:T(512)}, f32[512]{0:T(512)S(1)}, u32[]{:S(2)}) copy-start(f32[512]{0:T(512)S(1)} %broadcast_multiply_fusion.1) | copy-start | bytes 6148
  10.9 51.3 %copy-start.42 = (f32[512]{0:T(512)}, f32[512]{0:T(512)S(1)}, u32[]{:S(2)}) copy-start(f32[512]{0:T(512)S(1)} %fusion.109) | copy-start | bytes 6148
  11.0 51.3 %copy-start.40 = (f32[512]{0:T(512)}, f32[512]{0:T(512)S(1)}, u32[]{:S(2)}) copy-start(f32[512]{0:T(512)S(1)} %fusion.122) | copy-start | bytes 6148
  62.2 268.6 %reduce-scatter.19.cloned.1.call-start = ((), (), s32[]{:S(2)}) async-start(), calls=%async_computation.11 | async-start | bytes 3932160 | tf_op jit(solution)/shard_map/reduce_scatter | solution.py:158
  93.5 198.3 %copy-start.13 = (bf16[192,768]{0,1:T(8,128)(2,1)}, bf16[192,768]{0,1:T(8,128)(2,1)S(1)}, u32[]{:S(2)}) copy-start(bf16[192,768]{0,1:T(8,128)(2,1)S(1)} %all_gather.71) | copy-start | bytes 884740
  124.5 62.1 %copy-start.26 = (bf16[768,192]{1,0:T(8,128)(2,1)}, bf16[768,192]{1,0:T(8,128)(2,1)S(1)}, u32[]{:S(2)}) copy-start(bf16[768,192]{1,0:T(8,128)(2,1)S(1)} %all_gather.66) | copy-start | bytes 884740
  155.5 31.1 %copy-start.28 = (bf16[768,192]{1,0:T(8,128)(2,1)}, bf16[768,192]{1,0:T(8,128)(2,1)S(1)}, u32[]{:S(2)}) copy-start(bf16[768,192]{1,0:T(8,128)(2,1)S(1)} %all_gather.67) | copy-start | bytes 884740
  292.7 38.1 %copy-start.1 = (bf16[512,768]{1,0:T(8,128)(2,1)S(1)}, bf16[512,768]{1,0:T(8,128)(2,1)}, u32[]{:S(2)}) copy-start(bf16[512,768]{1,0:T(8,128)(2,1)} %param.22) | copy-start | bytes 2359300
  295.4 67.8 %all-gather.12.cloned.1.call-start = ((), (), s32[]{:S(2)}) async-start(), calls=%async_computation.13 | async-start | bytes 1327104 | tf_op jit(solution)/shard_map/all_gather | solution.py:88
  296.0 70.1 %all-gather.10.cloned.1.call-start = ((), (), s32[]{:S(2)}) async-start(), calls=%async_computation.12 | async-start | bytes 3932160 | tf_op jit(solution)/shard_map/all_gather | solution.py:163
  335.3 74.6 %all-gather.14.cloned.1.call-start = ((), (), s32[]{:S(2)}) async-start(), calls=%async_computation.14 | async-start | bytes 1327104 | tf_op jit(solution)/shard_map/all_gather | solution.py:90
  335.9 102.6 %all-gather.16.cloned.1.call-start = ((), (), s32[]{:S(2)}) async-start(), calls=%async_computation.16 | async-start | bytes 3932160 | tf_op jit(solution)/shard_map/all_gather | solution.py:183
  336.7 166.2 %reduce-scatter.23.cloned.1.call-start = ((), (), s32[]{:S(2)}) async-start(), calls=%async_computation.17 | async-start | bytes 3932160 | tf_op jit(solution)/shard_map/reduce_scatter | solution.py:191
  438.5 22.3 %copy-start.49 = (bf16[768,768]{1,0:T(8,128)(2,1)S(1)}, bf16[768,768]{1,0:T(8,128)(2,1)}, u32[]{:S(2)}) copy-start(bf16[768,768]{1,0:T(8,128)(2,1)} %all-gather.12.cloned.1.call-done) | copy-start | bytes 3538948
  464.8 78.5 %reduce-scatter.21.cloned.1.call-start = ((), (), s32[]{:S(2)}) async-start(), calls=%async_computation.15 | async-start | bytes 3932160 | tf_op jit(solution)/shard_map/reduce_scatter | solution.py:167
  464.8 7.2 copy-start.50
  476.1 101.8 %all-gather.18.cloned.1.call-start = ((), (), s32[]{:S(2)}) async-start(), calls=%async_computation.18 | async-start | bytes 3932160 | tf_op jit(solution)/shard_map/all_gather | solution.py:202
  547.3 30.7 %copy-start.18 = (bf16[4,24,8,512]{3,2,0,1:T(8,128)(2,1)S(1)}, bf16[4,24,8,512]{3,2,0,1:T(8,128)(2,1)}, u32[]{:S(2)}) copy-start(bf16[4,24,8,512]{3,2,0,1:T(8,128)(2,1)} %copy-done.17) | copy-start | bytes 2359300
  549.4 336.2 %reduce-scatter.37.cloned.1.call-start = ((), (), s32[]{:S(2)}) async-start(), calls=%async_computation.25 | async-start | bytes 884736
  549.5 32.6 %copy-start.14 = (bf16[192,768]{0,1:T(8,128)(2,1)S(1)}, bf16[192,768]{0,1:T(8,128)(2,1)}, u32[]{:S(2)}) copy-start(bf16[192,768]{0,1:T(8,128)(2,1)} %copy-done.13) | copy-start | bytes 884740
  582.1 6.8 copy-start.11
  582.1 314.7 %reduce-scatter.25.cloned.1.call-start = ((), (), s32[]{:S(2)}) async-start(), calls=%async_computation.19 | async-start | bytes 3932160 | tf_op jit(solution)/shard_map/reduce_scatter | solution.py:251
  596.7 7.2 copy-start
  661.5 7.2 copy-start
  725.8 7.2 copy-start
  790.1 7.2 copy-start
  858.8 111.9 %reduce-scatter.29.cloned.1.call-start = ((), (), s32[]{:S(2)}) async-start(), calls=%async_computation.21 | async-start | bytes 2654208 | tf_op jit(solution)/shard_map/reduce_scatter | solution.py:299
  866.7 7.7 copy-start.21
  866.7 7.7 copy-start.23
  866.7 7.7 copy-start.25
  866.7 176.5 %reduce-scatter.27.cloned.1.call-start = ((), (), s32[]{:S(2)}) async-start(), calls=%async_computation.20 | async-start | bytes 2654208 | tf_op jit(solution)/shard_map/reduce_scatter | solution.py:298
  874.3 234.8 %reduce-scatter.35.cloned.1.call-start = ((), (), s32[]{:S(2)}) async-start(), calls=%async_computation.24 | async-start | bytes 884736
  879.6 294.9 %reduce-scatter.33.cloned.1.call-start = ((), (), s32[]{:S(2)}) async-start(), calls=%async_computation.23 | async-start | bytes 884736
  879.7 18.4 %copy-start.2 = (bf16[512,768]{1,0:T(8,128)(2,1)S(1)}, bf16[512,768]{1,0:T(8,128)(2,1)}, u32[]{:S(2)}) copy-start(bf16[512,768]{1,0:T(8,128)(2,1)} %param.22) | copy-start | bytes 2359300
  879.7 18.4 %copy-start.33 = (f32[768]{0:T(1024)S(1)}, f32[768]{0:T(1024)}, u32[]{:S(2)}) copy-start(f32[768]{0:T(1024)} %copy-done.32) | copy-start | bytes 9220
  879.7 18.4 %copy-start.35 = (f32[512]{0:T(512)S(1)}, f32[512]{0:T(512)}, u32[]{:S(2)}) copy-start(f32[512]{0:T(512)} %copy-done.34) | copy-start | bytes 6148
  880.9 359.5 %reduce-scatter.31.cloned.1.call-start = ((), (), s32[]{:S(2)}) async-start(), calls=%async_computation.22 | async-start | bytes 884736
  882.3 17.4 %copy-start.43 = (f32[512]{0:T(512)S(1)}, f32[512]{0:T(512)}, u32[]{:S(2)}) copy-start(f32[512]{0:T(512)} %copy-done.42) | copy-start | bytes 6148
  882.3 17.4 %copy-start.41 = (f32[512]{0:T(512)S(1)}, f32[512]{0:T(512)}, u32[]{:S(2)}) copy-start(f32[512]{0:T(512)} %copy-done.40) | copy-start | bytes 6148
  884.0 17.8 %copy-start.44 = (bf16[768]{0:T(1024)(128)(2,1)S(1)}, bf16[768]{0:T(1024)(128)(2,1)}, u32[]{:S(2)}) copy-start(bf16[768]{0:T(1024)(128)(2,1)} %get-tuple-element.387) | copy-start | bytes 4612
  884.0 17.9 %copy-start.45 = (bf16[768]{0:T(1024)(128)(2,1)S(1)}, bf16[768]{0:T(1024)(128)(2,1)}, u32[]{:S(2)}) copy-start(bf16[768]{0:T(1024)(128)(2,1)} %get-tuple-element.316) | copy-start | bytes 4612
  884.0 72.3 %copy-start.5 = (f32[512,768]{1,0:T(8,128)S(1)}, f32[512,768]{1,0:T(8,128)}, u32[]{:S(2)}) copy-start(f32[512,768]{1,0:T(8,128)} %copy-done.4) | copy-start | bytes 4718596
  896.7 59.5 %copy-start.7 = (bf16[512,768]{1,0:T(8,128)(2,1)S(1)}, bf16[512,768]{1,0:T(8,128)(2,1)}, u32[]{:S(2)}) copy-start(bf16[512,768]{1,0:T(8,128)(2,1)} %reduce-scatter.25.cloned.1.call-done) | copy-start | bytes 2359300
  (26 other events, 66.4 us)
Sparse Core Ops, SparseCore 0:
  62.3 25.7 all-gather.7
  295.5 35.2 reduce-scatter.18
  464.9 37.9 reduce-scatter.22
  505.2 37.9 reduce-scatter.20
Sparse Core Ops, SparseCore 1:
  298.3 38.8 all-gather.11
  339.2 26.8 all-gather.9
  368.4 41.5 all-gather.13
  411.6 26.8 all-gather.15
  549.5 28.3 all-gather.17
  582.1 62.5 reduce-scatter.36
  858.9 37.8 reduce-scatter.24
  901.1 69.5 reduce-scatter.28
  975.0 68.2 reduce-scatter.26
  1047.5 61.6 reduce-scatter.34
  1112.9 61.6 reduce-scatter.32
  1178.8 61.6 reduce-scatter.30
where the time goes:
time: 1250 us
  waiting for transfers between devices  487 us (39%)
  matrix products  358 us (29%)
  blocking collectives  239 us (19%)
  other arithmetic  70.1 us (6%)
  local copies, waits for them, and re-layouts  42.9 us (3%)
  loops' own time  31.9 us (3%)
  between operations  18.4 us (1%)
    unnamed x20, waiting for transfers between devices  199 us
    dot_general x4, matrix products, backward_block(): jnp.einsum('hqk,qhd->khd', grad_raw, query_block, preferred_element_type=...  89.7 us
    dot_general x4, matrix products, backward_block(): jnp.einsum('hqk,khd->qhd', grad_raw, key_seq, preferred_element_type=f32)  83.1 us
    unnamed x2, blocking collectives  78.3 us
    reduce_scatter x1, waiting for transfers between devices, per_device(): lax.psum_scatter(grad_w_in, 'dp', scatter_dimension=0, tiled=True)  72.6 us
    all_gather x1, waiting for transfers between devices, per_device(): lax.all_gather(w_back, 'dp', axis=1, tiled=True)  36.3 us
    reduce_scatter x1, waiting for transfers between devices, per_device(): lax.psum_scatter(mlp_part, 'tensor', scatter_dimension=0, tiled=True)  35.9 us
    reduce_scatter x1, waiting for transfers between devices, per_device(): lax.psum_scatter(attn_part, 'tensor', scatter_dimension=0, tiled=True)  34.7 us
  transfers between devices with their start and end apart: 16, of which 13 were waited for; matrix products, arithmetic and copies ran while one was open for 26% of the time, Pallas kernels for 0%

commit v1 on v0

--- a/solution.py
+++ b/solution.py
@@ -6,6 +6,22 @@
 
 HEAD_DIM = 64
 EPSILON = 1e-12
+
+
+def collect(x, axis, dim):
+    ways, here, step = (lax.axis_size(axis), lax.axis_index(axis), x.shape[dim])
+    shape = [n * ways if d == dim else n for d, n in enumerate(x.shape)]
+    full = lax.dynamic_update_slice_in_dim(jnp.zeros(shape, x.dtype), x, here * step, axis=dim)
+    going_up = going_down = x
+    for far in range(1, ways // 2 + 1):
+        going_up = lax.ppermute(going_up, axis, [(d, (d + 1) % ways) for d in range(ways)])
+        full = lax.dynamic_update_slice_in_dim(full, going_up, (here - far) % ways * step, axis=dim)
+        if 2 * far < ways:
+            going_down = lax.ppermute(going_down, axis, [(d, (d - 1) % ways) for d in range(ways)])
+            full = lax.dynamic_update_slice_in_dim(
+                full, going_down, (here + far) % ways * step, axis=dim
+            )
+    return full
 
 
 def layer_norm(values, gain, shift):
@@ -180,7 +196,7 @@
     merged_back = jnp.concatenate([back_query, back_key, back_value], axis=1)
     upstream = cotangent.astype(f32)
     back_bias_term = jnp.sum(upstream, axis=0)
-    cot_rows = lax.all_gather(cotangent, "tensor", axis=0, tiled=True)
+    cot_rows = collect(cotangent, "tensor", 0)
     grad_w_back = contract_rows(hidden, cot_rows)
     grad_hidden = contract_cols(cot_rows, back_back)
     gelu_out, gelu_pull = jax.vjp(gelu_exact, pre)

time: 1250 us -> 1230 us (0.984)
  waiting for transfers between devices: 487 us -> 457 us
    all_gather x1 -> x0, waiting for transfers between devices: 28.5 us -> none  [per_device(): cot_rows = lax.all_gather(cotangent, 'tensor', axis=0, tiled=True)]
    ppermute x0 -> x3, waiting for transfers between devices: none -> 24.9 us  [the longest x2 24.9 us: collect(): lax.ppermute(going_up, axis, [(d, (d + 1) % ways) for d in range(ways)])]
    all_gather x1, waiting for transfers between devices: 36.3 us -> 16.2 us  [per_device(): lax.all_gather(w_back, 'dp', axis=1, tiled=True)]
    unnamed x134 -> x122, local copies, waits for them, and re-layouts: 28.6 us -> 27.2 us
    unnamed x20 -> x19, waiting for transfers between devices: 199 us -> 198 us
  transfers between devices with their start and end apart: 16 -> 18, of which waited for: 13 -> 12; matrix products, arithmetic and copies ran while one was open for 26% -> 27% of each run, Pallas kernels for 0% -> 0%
where the time goes in v1:
time: 1230 us
  waiting for transfers between devices  457 us (37%)
  matrix products  359 us (29%)
  blocking collectives  238 us (19%)
  other arithmetic  71 us (6%)
  local copies, waits for them, and re-layouts  49.7 us (4%)
  loops' own time  31.9 us (3%)
  between operations  18.3 us (1%)
    unnamed x19, waiting for transfers between devices  198 us
    dot_general x4, matrix products, backward_block(): jnp.einsum('hqk,qhd->khd', grad_raw, query_block, preferred_element_type=...  89.9 us
    dot_general x4, matrix products, backward_block(): jnp.einsum('hqk,khd->qhd', grad_raw, key_seq, preferred_element_type=f32)  83.1 us
    unnamed x2, blocking collectives  77.7 us
    reduce_scatter x1, waiting for transfers between devices, per_device(): lax.psum_scatter(grad_w_in, 'dp', scatter_dimension=0, tiled=True)  72.5 us
    reduce_scatter x1, waiting for transfers between devices, per_device(): lax.psum_scatter(mlp_part, 'tensor', scatter_dimension=0, tiled=True)  35.9 us
    reduce_scatter x1, waiting for transfers between devices, per_device(): lax.psum_scatter(attn_part, 'tensor', scatter_dimension=0, tiled=True)  34.8 us
    dot_general x4, matrix products, contract_cols(): lax.dot_general(left, right, (((1,), (1,)), ((), ())), preferred_element_...  33.2 us
  transfers between devices with their start and end apart: 18, of which 12 were waited for; matrix products, arithmetic and copies ran while one was open for 27% of the time, Pallas kernels for 0%

profile of v1, /device:TPU:0, one launch (start us, length us, event | category | flops | bytes accessed | tf_op | source)
XLA Modules:
  0.0 1228.0 jit_solution(13960310975743180764)
XLA Ops:
  19.7 39.4 %all-reduce.18 = (bf16[768]{0:T(1024)(128)(2,1)S(1)}, bf16[768]{0:T(1024)(128)(2,1)S(1)}, bf16[768]{0:T(1024)(128)(2,1)S(1)}, bf16[768]{0:T(1024)(128)(2,1)S(1)}...) all-reduce(bf16[768]{0:T(1024)(128)(2,1)S(1)} %dynamic-update-slice, ...), channel_id=1, replica_groups=mesh['dp'=8,'tensor'=4] {'dp'}, use_global_device_ids=true, to_apply=%add.1 | all-reduce | flops 6144 | bytes 24576
  61.8 31.0 %all_gather.68 = bf16[192,768]{0,1:T(8,128)(2,1)S(1)} all-gather(bf16[192,96]{0,1:T(8,128)(2,1)S(1)} %copy.44), channel_id=1, replica_groups=mesh['dp'=8,'tensor'=4] {'dp'}, dimensions={1}, use_global_device_ids=true | all-gather | bytes 331776 | tf_op jit(solution)/shard_map/all_gather | solution.py:100
  92.8 31.0 %all_gather.63 = bf16[768,192]{1,0:T(8,128)(2,1)S(1)} all-gather(bf16[96,192]{1,0:T(8,128)(2,1)S(1)} %copy-done.29), channel_id=1, replica_groups=mesh['dp'=8,'tensor'=4] {'dp'}, dimensions={0}, use_global_device_ids=true | all-gather | bytes 331776 | tf_op jit(solution)/shard_map/all_gather | solution.py:95
  123.8 31.0 %all_gather.64 = bf16[768,192]{1,0:T(8,128)(2,1)S(1)} all-gather(bf16[96,192]{1,0:T(8,128)(2,1)S(1)} %copy-done.30), channel_id=1, replica_groups=mesh['dp'=8,'tensor'=4] {'dp'}, dimensions={0}, use_global_device_ids=true | all-gather | bytes 331776 | tf_op jit(solution)/shard_map/all_gather | solution.py:97
  154.8 31.1 %all_gather.65 = bf16[768,192]{1,0:T(8,128)(2,1)S(1)} all-gather(bf16[96,192]{1,0:T(8,128)(2,1)S(1)} %copy-done.31), channel_id=1, replica_groups=mesh['dp'=8,'tensor'=4] {'dp'}, dimensions={0}, use_global_device_ids=true | all-gather | bytes 331776 | tf_op jit(solution)/shard_map/all_gather | solution.py:98
  191.5 98.6 %while.30 = (s32[]{:T(128)}, bf16[4,512,192]{1,2,0:T(8,128)(2,1)}, f32[4,3,512]{2,1,0:T(4,128)S(1)}, s32[4]{0:T(128)S(1)}, s32[1,2048]{1,0:T(1,128)S(1)}, /*inde...) while((s32[]{:T(128)}, bf16[4,512,192]{1,2,0:T(8,128)(2,1)}, ...), condition=%wide.region_5.6_spmd, body=%wide.region_2.5_spmd.sunk | while | flops 844200448 | bytes 44372400 | solution.py:171
  202.0 6.8 fusion.179
  208.8 6.7 fusion.180
  226.7 6.8 fusion.179
  233.4 6.7 fusion.180
  251.3 6.8 fusion.179
  258.1 6.7 fusion.180
  276.0 6.8 fusion.179
  282.7 6.7 fusion.180
  295.9 34.8 %reduce-scatter.19.cloned.1.call-done = bf16[512,768]{1,0:T(8,128)(2,1)} async-done(((bf16[2048,768]{1,0:T(8,128)(2,1)}), bf16[512,768]{1,0:T(8,128)(2,1)}) %reduce-scatter.19.cloned.1.call-update) | async-done | bytes 786448 | tf_op jit(solution)/shard_map/reduce_scatter | solution.py:174
  337.2 24.9 %collective-permute-done = bf16[512,768]{1,0:T(8,128)(2,1)} collective-permute-done((bf16[512,768]{1,0:T(8,128)(2,1)}, bf16[512,768]{1,0:T(8,128)(2,1)}, u32[]{:S(2)}, u32[]{:S(2)}) %collective-permute-start) | collective-permute-done | bytes 786464 | tf_op jit(solution)/shard_map/ppermute | solution.py:17
  362.0 26.3 %all-gather = bf16[8,1,384]{2,1,0:T(2,128)(2,1)S(1)} all-gather(bf16[1,1,384]{2,1,0:T(2,128)(2,1)S(1)} %reshape.282), channel_id=1, replica_groups=mesh['dp'=8,'tensor'=4] {'dp'}, dimensions={0}, use_global_device_ids=true | all-gather | bytes 6912 | tf_op jit(solution)/shard_map/all_gather | solution.py:105
  398.2 7.6 fusion.136
  405.8 16.2 %all-gather.13.cloned.1.call-done = bf16[768,768]{0,1:T(8,128)(2,1)} async-done(((bf16[768,96]{0,1:T(8,128)(2,1)}), bf16[768,768]{0,1:T(8,128)(2,1)}) %all-gather.13.cloned.1.call-update) | async-done | bytes 1179664 | tf_op jit(solution)/shard_map/all_gather | solution.py:106
  421.9 20.5 %fusion.128 = (bf16[768]{0:T(1024)(128)(2,1)}, bf16[2048,768]{1,0:T(8,128)(2,1)S(1)}, f32[2048,768]{1,0:T(8,128)}) fusion(f32[2048,768]{1,0:T(8,128)} %fusion.136, f32[768]{0:T(1024)S(1)} %dynamic-slice_convert_fusion, bf16[2048,768]{1,0:T(8,128)(2,1)} %constant_dynamic-update-slice_fusion, bf16[768,768]{0,1:T(8,128)(2,1)} %all-gather.13.cloned.1.call-done), kind=kOutput, calls=%fused_computation.157 | convolution fusion | flops 2532310272 | bytes 20058624 | tf_op jit(solution)/shard_map/dot_general | solution.py:44
  460.8 23.8 %reduce-scatter.23.cloned.1.call-done = bf16[512,768]{1,0:T(8,128)(2,1)} async-done(((bf16[2048,768]{1,0:T(8,128)(2,1)}), bf16[512,768]{1,0:T(8,128)(2,1)}) %reduce-scatter.23.cloned.1.call-update) | async-done | bytes 786448 | tf_op jit(solution)/shard_map/reduce_scatter | solution.py:207
  489.1 35.9 %reduce-scatter.21.cloned.1.call-done = bf16[512,768]{1,0:T(8,128)(2,1)} async-done(((bf16[2048,768]{1,0:T(8,128)(2,1)}), bf16[512,768]{1,0:T(8,128)(2,1)}) %reduce-scatter.21.cloned.1.call-update) | async-done | bytes 786448 | tf_op jit(solution)/shard_map/reduce_scatter | solution.py:183
  531.2 28.6 %all-gather.15.cloned.1.call-done = bf16[2048,768]{1,0:T(8,128)(2,1)} async-done(((bf16[512,768]{1,0:T(8,128)(2,1)}), bf16[2048,768]{1,0:T(8,128)(2,1)}) %all-gather.15.cloned.1.call-update) | async-done | bytes 3145744 | tf_op jit(solution)/shard_map/all_gather | solution.py:218
  570.8 258.2 %while.31 = (s32[]{:T(128)}, f32[1,2048,3,64]{1,3,2,0:T(8,128)}, f32[1,2048,3,64]{1,3,2,0:T(8,128)}, f32[4,512,3,64]{1,3,2,0:T(8,128)}, s32[4]{0:T(128)S(1)}, /*...) while((s32[]{:T(128)}, f32[1,2048,3,64]{1,3,2,0:T(8,128)}, ...), condition=%wide.region_15.16_spmd, body=%wide.region_13.15_spmd.sunk | while | flops 2096897024 | bytes 208079408 | solution.py:254
  578.6 7.2 fusion.194
  592.2 20.9 %fusion.195 = f32[4,512,3,64]{1,3,2,0:T(8,128)} fusion(f32[4,512,3,64]{1,3,2,0:T(8,128)} %get-tuple-element.597, s32[]{:T(128)S(6)} %copy.87, f32[3,512,2048]{2,1,0:T(8,128)} %fusion.191, f32[3,512,2048]{2,1,0:T(8,128)} %copy-done, f32[3,512]{1,0:T(4,128)S(1)} %dynamic-slice_bitcast_fusion.2, pred[512,2048]{1,0:T(8,128)(4,1)S(1)} %broadcast_compare_fusion.5, ...), kind=kOutput, calls=%fused_computation.44.clone.1 | convolution fusion | flops 437259776 | bytes 53624836 | tf_op jit(solution)/shard_map/while/body/eval_jaxpr/hqk,khd->qhd/dot_general | solution.py:236
  613.1 22.6 %fusion.193 = f32[1,2048,3,64]{1,3,2,0:T(8,128)} fusion(f32[3,512,2048]{2,1,0:T(8,128)} %fusion.191, f32[3,512,2048]{2,1,0:T(8,128)} %copy-done, f32[3,512]{1,0:T(4,128)S(1)} %dynamic-slice_bitcast_fusion.2, pred[512,2048]{1,0:T(8,128)(4,1)S(1)} %broadcast_compare_fusion.5, f32[1,2048,3,64]{1,3,2,0:T(8,128)} %get-tuple-element.595, ...), kind=kOutput, calls=%fused_computation.39.clone.1 | convolution fusion | flops 437652992 | bytes 55787524 | tf_op jit(solution)/shard_map/while/body/eval_jaxpr/hqk,qhd->khd/dot_general | solution.py:237
  643.4 7.2 fusion.194
  650.5 6.3 fusion.191
  656.9 20.7 %fusion.195 = f32[4,512,3,64]{1,3,2,0:T(8,128)} fusion(f32[4,512,3,64]{1,3,2,0:T(8,128)} %get-tuple-element.597, s32[]{:T(128)S(6)} %copy.87, f32[3,512,2048]{2,1,0:T(8,128)} %fusion.191, f32[3,512,2048]{2,1,0:T(8,128)} %copy-done, f32[3,512]{1,0:T(4,128)S(1)} %dynamic-slice_bitcast_fusion.2, pred[512,2048]{1,0:T(8,128)(4,1)S(1)} %broadcast_compare_fusion.5, ...), kind=kOutput, calls=%fused_computation.44.clone.1 | convolution fusion | flops 437259776 | bytes 53624836 | tf_op jit(solution)/shard_map/while/body/eval_jaxpr/hqk,khd->qhd/dot_general | solution.py:236
  677.6 22.5 %fusion.193 = f32[1,2048,3,64]{1,3,2,0:T(8,128)} fusion(f32[3,512,2048]{2,1,0:T(8,128)} %fusion.191, f32[3,512,2048]{2,1,0:T(8,128)} %copy-done, f32[3,512]{1,0:T(4,128)S(1)} %dynamic-slice_bitcast_fusion.2, pred[512,2048]{1,0:T(8,128)(4,1)S(1)} %broadcast_compare_fusion.5, f32[1,2048,3,64]{1,3,2,0:T(8,128)} %get-tuple-element.595, ...), kind=kOutput, calls=%fused_computation.39.clone.1 | convolution fusion | flops 437652992 | bytes 55787524 | tf_op jit(solution)/shard_map/while/body/eval_jaxpr/hqk,qhd->khd/dot_general | solution.py:237
  707.7 7.2 fusion.194
  721.2 20.7 %fusion.195 = f32[4,512,3,64]{1,3,2,0:T(8,128)} fusion(f32[4,512,3,64]{1,3,2,0:T(8,128)} %get-tuple-element.597, s32[]{:T(128)S(6)} %copy.87, f32[3,512,2048]{2,1,0:T(8,128)} %fusion.191, f32[3,512,2048]{2,1,0:T(8,128)} %copy-done, f32[3,512]{1,0:T(4,128)S(1)} %dynamic-slice_bitcast_fusion.2, pred[512,2048]{1,0:T(8,128)(4,1)S(1)} %broadcast_compare_fusion.5, ...), kind=kOutput, calls=%fused_computation.44.clone.1 | convolution fusion | flops 437259776 | bytes 53624836 | tf_op jit(solution)/shard_map/while/body/eval_jaxpr/hqk,khd->qhd/dot_general | solution.py:236
  741.9 22.5 %fusion.193 = f32[1,2048,3,64]{1,3,2,0:T(8,128)} fusion(f32[3,512,2048]{2,1,0:T(8,128)} %fusion.191, f32[3,512,2048]{2,1,0:T(8,128)} %copy-done, f32[3,512]{1,0:T(4,128)S(1)} %dynamic-slice_bitcast_fusion.2, pred[512,2048]{1,0:T(8,128)(4,1)S(1)} %broadcast_compare_fusion.5, f32[1,2048,3,64]{1,3,2,0:T(8,128)} %get-tuple-element.595, ...), kind=kOutput, calls=%fused_computation.39.clone.1 | convolution fusion | flops 437652992 | bytes 55787524 | tf_op jit(solution)/shard_map/while/body/eval_jaxpr/hqk,qhd->khd/dot_general | solution.py:237
  772.1 7.2 fusion.194
  779.3 6.3 fusion.191
  785.6 20.8 %fusion.195 = f32[4,512,3,64]{1,3,2,0:T(8,128)} fusion(f32[4,512,3,64]{1,3,2,0:T(8,128)} %get-tuple-element.597, s32[]{:T(128)S(6)} %copy.87, f32[3,512,2048]{2,1,0:T(8,128)} %fusion.191, f32[3,512,2048]{2,1,0:T(8,128)} %copy-done, f32[3,512]{1,0:T(4,128)S(1)} %dynamic-slice_bitcast_fusion.2, pred[512,2048]{1,0:T(8,128)(4,1)S(1)} %broadcast_compare_fusion.5, ...), kind=kOutput, calls=%fused_computation.44.clone.1 | convolution fusion | flops 437259776 | bytes 53624836 | tf_op jit(solution)/shard_map/while/body/eval_jaxpr/hqk,khd->qhd/dot_general | solution.py:236
  806.4 22.5 %fusion.193 = f32[1,2048,3,64]{1,3,2,0:T(8,128)} fusion(f32[3,512,2048]{2,1,0:T(8,128)} %fusion.191, f32[3,512,2048]{2,1,0:T(8,128)} %copy-done, f32[3,512]{1,0:T(4,128)S(1)} %dynamic-slice_bitcast_fusion.2, pred[512,2048]{1,0:T(8,128)(4,1)S(1)} %broadcast_compare_fusion.5, f32[1,2048,3,64]{1,3,2,0:T(8,128)} %get-tuple-element.595, ...), kind=kOutput, calls=%fused_computation.39.clone.1 | convolution fusion | flops 437652992 | bytes 55787524 | tf_op jit(solution)/shard_map/while/body/eval_jaxpr/hqk,qhd->khd/dot_general | solution.py:237
  839.0 6.9 fusion.137
  846.0 7.7 fusion.114
  867.8 9.1 reduce-scatter.25.cloned.1.call-done
  882.0 10.3 all-reduce.19
  892.3 38.3 %all-reduce.17 = (f32[768]{0:T(1024)S(1)}, f32[768]{0:T(1024)S(1)}, f32[768]{0:T(1024)S(1)}, f32[768]{0:T(1024)S(1)}, f32[768]{0:T(1024)S(1)}, /*index=5*/f32[76...) all-reduce(bf16[768]{0:T(1024)(128)(2,1)S(1)} %get-tuple-element.37, ...), channel_id=6, replica_groups=mesh['dp'=8,'tensor'=4] {'dp'}, use_global_device_ids=true, to_apply=%region_21.22.clone | all-reduce | flops 9216 | bytes 55296
  937.6 13.4 %reduce-scatter.29.cloned.1.call-done = f32[768,96]{0,1:T(8,128)} async-done(((f32[768,768]{0,1:T(8,128)}), f32[768,96]{0,1:T(8,128)}) %reduce-scatter.29.cloned.1.call-update) | async-done | bytes 294928 | tf_op jit(solution)/shard_map/reduce_scatter | solution.py:315
  951.0 72.5 %reduce-scatter.27.cloned.1.call-done = f32[96,768]{1,0:T(8,128)} async-done(((f32[768,768]{1,0:T(8,128)}), f32[96,768]{1,0:T(8,128)}) %reduce-scatter.27.cloned.1.call-update) | async-done | bytes 294928 | tf_op jit(solution)/shard_map/reduce_scatter | solution.py:314
  1023.5 65.9 %reduce-scatter.35.cloned.1.call-done = f32[96,192]{1,0:T(8,128)} async-done(((f32[768,192]{1,0:T(8,128)}), f32[96,192]{1,0:T(8,128)}) %reduce-scatter.35.cloned.1.call-update) | async-done | bytes 73744
  1089.4 65.4 %reduce-scatter.33.cloned.1.call-done = f32[96,192]{1,0:T(8,128)} async-done(((f32[768,192]{1,0:T(8,128)}), f32[96,192]{1,0:T(8,128)}) %reduce-scatter.33.cloned.1.call-update) | async-done | bytes 73744
  1154.8 65.9 %reduce-scatter.31.cloned.1.call-done = f32[96,192]{1,0:T(8,128)} async-done(((f32[768,192]{1,0:T(8,128)}), f32[96,192]{1,0:T(8,128)}) %reduce-scatter.31.cloned.1.call-update) | async-done | bytes 73744
  (292 shorter events, 172.3 us)
Async XLA Ops:
  8.0 53.6 %copy-start.32 = (bf16[192,96]{1,0:T(8,128)(2,1)S(1)}, bf16[192,96]{1,0:T(8,128)(2,1)}, u32[]{:S(2)}) copy-start(bf16[192,96]{1,0:T(8,128)(2,1)} %param.32) | copy-start | bytes 110596
  8.0 84.8 %copy-start.29 = (bf16[96,192]{1,0:T(8,128)(2,1)S(1)}, bf16[96,192]{1,0:T(8,128)(2,1)}, u32[]{:S(2)}) copy-start(bf16[96,192]{1,0:T(8,128)(2,1)} %param.27) | copy-start | bytes 110596
  8.0 115.7 %copy-start.30 = (bf16[96,192]{1,0:T(8,128)(2,1)S(1)}, bf16[96,192]{1,0:T(8,128)(2,1)}, u32[]{:S(2)}) copy-start(bf16[96,192]{1,0:T(8,128)(2,1)} %param.29) | copy-start | bytes 110596
  8.1 146.8 %copy-start.31 = (bf16[96,192]{1,0:T(8,128)(2,1)S(1)}, bf16[96,192]{1,0:T(8,128)(2,1)}, u32[]{:S(2)}) copy-start(bf16[96,192]{1,0:T(8,128)(2,1)} %param.30) | copy-start | bytes 110596
  8.1 177.9 %all-gather.7.cloned.1.call-start = ((), (), s32[]{:S(2)}) async-start(), calls=%async_computation.10 | async-start | bytes 3932160 | tf_op jit(solution)/shard_map/all_gather | solution.py:124
  9.4 114.3 %copy-start.27 = (f32[512]{0:T(512)}, f32[512]{0:T(512)S(1)}, u32[]{:S(2)}) copy-start(f32[512]{0:T(512)S(1)} %broadcast_multiply_fusion.1) | copy-start | bytes 6148
  10.9 48.2 %copy-start.35 = (f32[512]{0:T(512)}, f32[512]{0:T(512)S(1)}, u32[]{:S(2)}) copy-start(f32[512]{0:T(512)S(1)} %fusion.109) | copy-start | bytes 6148
  11.0 50.6 %copy-start.33 = (f32[512]{0:T(512)}, f32[512]{0:T(512)S(1)}, u32[]{:S(2)}) copy-start(f32[512]{0:T(512)S(1)} %fusion.122) | copy-start | bytes 6148
  59.1 64.7 %copy-start.25 = (f32[768]{0:T(1024)}, f32[768]{0:T(1024)S(1)}, u32[]{:S(2)}) copy-start(f32[768]{0:T(1024)S(1)} %convert_element_type.172) | copy-start | bytes 9220
  61.5 269.2 %reduce-scatter.19.cloned.1.call-start = ((), (), s32[]{:S(2)}) async-start(), calls=%async_computation.11 | async-start | bytes 3932160 | tf_op jit(solution)/shard_map/reduce_scatter | solution.py:174
  92.8 198.8 %copy-start.12 = (bf16[192,768]{0,1:T(8,128)(2,1)}, bf16[192,768]{0,1:T(8,128)(2,1)S(1)}, u32[]{:S(2)}) copy-start(bf16[192,768]{0,1:T(8,128)(2,1)S(1)} %all_gather.68) | copy-start | bytes 884740
  123.8 67.0 %copy-start.19 = (bf16[768,192]{1,0:T(8,128)(2,1)}, bf16[768,192]{1,0:T(8,128)(2,1)S(1)}, u32[]{:S(2)}) copy-start(bf16[768,192]{1,0:T(8,128)(2,1)S(1)} %all_gather.63) | copy-start | bytes 884740
  154.8 36.0 %copy-start.21 = (bf16[768,192]{1,0:T(8,128)(2,1)}, bf16[768,192]{1,0:T(8,128)(2,1)S(1)}, u32[]{:S(2)}) copy-start(bf16[768,192]{1,0:T(8,128)(2,1)S(1)} %all_gather.64) | copy-start | bytes 884740
  292.5 38.2 %copy-start.1 = (bf16[512,768]{1,0:T(8,128)(2,1)S(1)}, bf16[512,768]{1,0:T(8,128)(2,1)}, u32[]{:S(2)}) copy-start(bf16[512,768]{1,0:T(8,128)(2,1)} %param.22) | copy-start | bytes 2359300
  295.3 102.9 %all-gather.11.cloned.1.call-start = ((), (), s32[]{:S(2)}) async-start(), calls=%async_computation.13 | async-start | bytes 1327104 | tf_op jit(solution)/shard_map/all_gather | solution.py:104
  295.9 102.3 %all-gather.9.cloned.1.call-start = ((), (), s32[]{:S(2)}) async-start(), calls=%async_computation.12 | async-start | bytes 3932160 | tf_op jit(solution)/shard_map/all_gather | solution.py:179
  295.9 66.1 %copy-start.42 = (bf16[384]{0:T(512)(128)(2,1)S(1)}, bf16[384]{0:T(512)(128)(2,1)}, u32[]{:S(2)}) copy-start(bf16[384]{0:T(512)(128)(2,1)} %param.37) | copy-start | bytes 2308
  335.2 86.7 %all-gather.13.cloned.1.call-start = ((), (), s32[]{:S(2)}) async-start(), calls=%async_computation.14 | async-start | bytes 1327104 | tf_op jit(solution)/shard_map/all_gather | solution.py:106
  335.3 26.8 %collective-permute-start = (bf16[512,768]{1,0:T(8,128)(2,1)}, bf16[512,768]{1,0:T(8,128)(2,1)}, u32[]{:S(2)}, u32[]{:S(2)}) collective-permute-start(bf16[512,768]{1,0:T(8,128)(2,1)} %param.23), channel_id=1, source_target_pairs={{0,1},{1,2},{2,3},{3,0},{4,5},{5,6},{6,7},{7,4},{8,9},{9,10},{10,1... | collective-permute-start | bytes 2359304 | tf_op jit(solution)/shard_map/ppermute | solution.py:17
  335.8 148.8 %reduce-scatter.23.cloned.1.call-start = ((), (), s32[]{:S(2)}) async-start(), calls=%async_computation.16 | async-start | bytes 3932160 | tf_op jit(solution)/shard_map/reduce_scatter | solution.py:207
  335.8 58.2 %collective-permute-start.1 = (bf16[512,768]{1,0:T(8,128)(2,1)}, bf16[512,768]{1,0:T(8,128)(2,1)}, u32[]{:S(2)}, u32[]{:S(2)}) collective-permute-start(bf16[512,768]{1,0:T(8,128)(2,1)} %param.23), channel_id=1, source_target_pairs={{0,3},{1,0},{2,1},{3,2},{4,7},{5,4},{6,5},{7,6},{8,11},{9,8},{10,9... | collective-permute-start | bytes 2359304 | tf_op jit(solution)/shard_map/ppermute | solution.py:20
  362.0 34.1 %collective-permute-start.2 = (bf16[512,768]{1,0:T(8,128)(2,1)}, bf16[512,768]{1,0:T(8,128)(2,1)}, u32[]{:S(2)}, u32[]{:S(2)}) collective-permute-start(bf16[512,768]{1,0:T(8,128)(2,1)} %collective-permute-done), channel_id=1, source_target_pairs={{0,1},{1,2},{2,3},{3,0},{4,5},{5,6},{6,7},{7,4},{8,9},{9,10},{10,1... | collective-permute-start | bytes 2359304 | tf_op jit(solution)/shard_map/ppermute | solution.py:17
  421.9 22.2 %copy-start.43 = (bf16[768,768]{1,0:T(8,128)(2,1)S(1)}, bf16[768,768]{1,0:T(8,128)(2,1)}, u32[]{:S(2)}) copy-start(bf16[768,768]{1,0:T(8,128)(2,1)} %all-gather.11.cloned.1.call-done) | copy-start | bytes 3538948
  448.1 76.8 %reduce-scatter.21.cloned.1.call-start = ((), (), s32[]{:S(2)}) async-start(), calls=%async_computation.15 | async-start | bytes 3932160 | tf_op jit(solution)/shard_map/reduce_scatter | solution.py:183
  448.2 7.9 copy-start.44
  460.1 99.7 %all-gather.15.cloned.1.call-start = ((), (), s32[]{:S(2)}) async-start(), calls=%async_computation.17 | async-start | bytes 3932160 | tf_op jit(solution)/shard_map/all_gather | solution.py:218
  529.0 30.8 %copy-start.17 = (bf16[4,24,8,512]{3,2,0,1:T(8,128)(2,1)S(1)}, bf16[4,24,8,512]{3,2,0,1:T(8,128)(2,1)}, u32[]{:S(2)}) copy-start(bf16[4,24,8,512]{3,2,0,1:T(8,128)(2,1)} %copy-done.16) | copy-start | bytes 2359300
  531.2 335.0 %reduce-scatter.37.cloned.1.call-start = ((), (), s32[]{:S(2)}) async-start(), calls=%async_computation.24 | async-start | bytes 884736
  531.2 32.8 %copy-start.13 = (bf16[192,768]{0,1:T(8,128)(2,1)S(1)}, bf16[192,768]{0,1:T(8,128)(2,1)}, u32[]{:S(2)}) copy-start(bf16[192,768]{0,1:T(8,128)(2,1)} %copy-done.12) | copy-start | bytes 884740
  564.0 312.9 %reduce-scatter.25.cloned.1.call-start = ((), (), s32[]{:S(2)}) async-start(), calls=%async_computation.18 | async-start | bytes 3932160 | tf_op jit(solution)/shard_map/reduce_scatter | solution.py:267
  578.6 7.2 copy-start
  643.3 7.2 copy-start
  772.1 7.2 copy-start
  838.9 112.0 %reduce-scatter.29.cloned.1.call-start = ((), (), s32[]{:S(2)}) async-start(), calls=%async_computation.20 | async-start | bytes 2654208 | tf_op jit(solution)/shard_map/reduce_scatter | solution.py:315
  845.9 177.5 %reduce-scatter.27.cloned.1.call-start = ((), (), s32[]{:S(2)}) async-start(), calls=%async_computation.19 | async-start | bytes 2654208 | tf_op jit(solution)/shard_map/reduce_scatter | solution.py:314
  853.7 235.6 %reduce-scatter.35.cloned.1.call-start = ((), (), s32[]{:S(2)}) async-start(), calls=%async_computation.23 | async-start | bytes 884736
  859.8 18.4 %copy-start.2 = (bf16[512,768]{1,0:T(8,128)(2,1)S(1)}, bf16[512,768]{1,0:T(8,128)(2,1)}, u32[]{:S(2)}) copy-start(bf16[512,768]{1,0:T(8,128)(2,1)} %param.22) | copy-start | bytes 2359300
  859.8 18.4 %copy-start.26 = (f32[768]{0:T(1024)S(1)}, f32[768]{0:T(1024)}, u32[]{:S(2)}) copy-start(f32[768]{0:T(1024)} %copy-done.25) | copy-start | bytes 9220
  859.8 18.4 %copy-start.28 = (f32[512]{0:T(512)S(1)}, f32[512]{0:T(512)}, u32[]{:S(2)}) copy-start(f32[512]{0:T(512)} %copy-done.27) | copy-start | bytes 6148
  859.9 294.9 %reduce-scatter.33.cloned.1.call-start = ((), (), s32[]{:S(2)}) async-start(), calls=%async_computation.22 | async-start | bytes 884736
  861.1 18.8 %copy-start.36 = (f32[512]{0:T(512)S(1)}, f32[512]{0:T(512)}, u32[]{:S(2)}) copy-start(f32[512]{0:T(512)} %copy-done.35) | copy-start | bytes 6148
  861.1 18.8 %copy-start.34 = (f32[512]{0:T(512)S(1)}, f32[512]{0:T(512)}, u32[]{:S(2)}) copy-start(f32[512]{0:T(512)} %copy-done.33) | copy-start | bytes 6148
  861.1 359.5 %reduce-scatter.31.cloned.1.call-start = ((), (), s32[]{:S(2)}) async-start(), calls=%async_computation.21 | async-start | bytes 884736
  863.3 18.7 %copy-start.37 = (bf16[768]{0:T(1024)(128)(2,1)S(1)}, bf16[768]{0:T(1024)(128)(2,1)}, u32[]{:S(2)}) copy-start(bf16[768]{0:T(1024)(128)(2,1)} %get-tuple-element.387) | copy-start | bytes 4612
  863.3 18.7 %copy-start.38 = (bf16[768]{0:T(1024)(128)(2,1)S(1)}, bf16[768]{0:T(1024)(128)(2,1)}, u32[]{:S(2)}) copy-start(bf16[768]{0:T(1024)(128)(2,1)} %get-tuple-element.401) | copy-start | bytes 4612
  863.3 18.7 %copy-start.39 = (bf16[768]{0:T(1024)(128)(2,1)S(1)}, bf16[768]{0:T(1024)(128)(2,1)}, u32[]{:S(2)}) copy-start(bf16[768]{0:T(1024)(128)(2,1)} %get-tuple-element.316) | copy-start | bytes 4612
  863.3 72.6 %copy-start.5 = (f32[512,768]{1,0:T(8,128)S(1)}, f32[512,768]{1,0:T(8,128)}, u32[]{:S(2)}) copy-start(f32[512,768]{1,0:T(8,128)} %copy-done.4) | copy-start | bytes 4718596
  876.9 59.0 %copy-start.7 = (bf16[512,768]{1,0:T(8,128)(2,1)S(1)}, bf16[512,768]{1,0:T(8,128)(2,1)}, u32[]{:S(2)}) copy-start(bf16[512,768]{1,0:T(8,128)(2,1)} %reduce-scatter.25.cloned.1.call-done) | copy-start | bytes 2359300
  (22 other events, 56.0 us)
Sparse Core Ops, SparseCore 0:
  61.6 25.7 all-gather.6
  295.4 35.2 reduce-scatter.18
  531.3 28.5 all-gather.14
Sparse Core Ops, SparseCore 1:
  297.9 38.8 all-gather.10
  338.8 38.4 all-gather.8
  379.5 42.3 all-gather.12
  448.2 36.3 reduce-scatter.22
  487.1 37.8 reduce-scatter.20
  564.1 62.5 reduce-scatter.36
  839.0 37.8 reduce-scatter.24
  881.2 69.7 reduce-scatter.28
  955.3 68.1 reduce-scatter.26
  1027.7 61.6 reduce-scatter.34
  1093.1 61.6 reduce-scatter.32
  1159.0 61.5 reduce-scatter.30
